TPU v7x, 32 devices: a whole 2x2x4 slice. The times are simulated.
32 devices in a mesh: groups: 2 (over x), tensor: 16 (over z, y, core).
Axes of the slice: x: 2, y: 2, z: 4, core: 2. Of those that a mesh axis runs over, the one named last changes fastest.
Arguments:
- teacher_in: bfloat16 [1024, 5376], P(('groups', 'tensor')), parts along dimension 0, may hold values from -6 to 6
- gate_weight: bfloat16 [21504, 5376], P('tensor'), may hold values from -0.078125 to 0.078125
- up_weight: bfloat16 [21504, 5376], P('tensor'), may hold values from -0.078125 to 0.078125
- down_weight: bfloat16 [21504, 5376], P('tensor'), may hold values from -0.0546875 to 0.0546875
- post_gain: bfloat16 [5376], replicated, may hold values from 0.099609375 to 1.8984375
- student_in: bfloat16 [1024, 2560], P(('groups', 'tensor')), parts along dimension 0, may hold values from -6 to 6
- proj_weight: bfloat16 [5376, 2560], P('tensor'), may hold values from -0.125 to 0.125
Outputs:
- loss_value: float32 [2], P('groups'), parts along dimension 0
- proj_grad: float32 [10752, 2560], P(('groups', 'tensor')), parts along dimension 0
- student_grad: bfloat16 [1024, 2560], P(('groups', 'tensor')), parts along dimension 0
There are 2 independent parts, one for each index of `groups`. A program takes and returns all parts, laid end to end along the dimension named above; an argument that names none is the same for every part. Nothing has to cross between parts.
All inputs are finite; a program needn't handle non-finite values.
Results may differ from a plain program's by a relative error of at most 0.0051.
Values may be sent and summed in bfloat16 or wider, within the bound.
A program may use at most 128 MiB of HBM per device.

v0:
```python
import jax
import jax.numpy as jnp
from jax import lax
from jax.sharding import PartitionSpec as P

epsilon = 1e-06


def local(teacher_in, gate_weight, up_weight, down_weight, post_gain, student_in, proj_weight):
    width_count = lax.axis_size("tensor")
    gains = post_gain.astype(jnp.float32)
    contract_last = (((1,), (1,)), ((), ()))
    block_rows = lax.all_gather(teacher_in, "tensor", axis=0, tiled=True)
    gate_value = lax.dot_general(
        block_rows, gate_weight, contract_last, preferred_element_type=jnp.float32
    )
    lift_value = lax.dot_general(
        block_rows, up_weight, contract_last, preferred_element_type=jnp.float32
    )
    hidden = (jax.nn.gelu(gate_value, approximate=True) * lift_value).astype(jnp.bfloat16)
    student_all = lax.all_gather(student_in, "tensor", axis=0, tiled=True)
    row_block = hidden
    ffn_out = lax.psum_scatter(
        jnp.dot(row_block, down_weight, preferred_element_type=jnp.float32),
        "tensor",
        scatter_dimension=0,
        tiled=True,
    )
    inv_norm = lax.rsqrt(jnp.mean(ffn_out * ffn_out, axis=-1, keepdims=True) + epsilon)
    target_rows = (teacher_in.astype(jnp.float32) + ffn_out * inv_norm * gains).astype(jnp.bfloat16)
    target = lax.all_to_all(target_rows, "tensor", split_axis=1, concat_axis=0, tiled=True)
    projected = lax.dot_general(
        student_all, proj_weight, contract_last, preferred_element_type=jnp.float32
    )
    difference = projected - target.astype(jnp.float32)
    total_error = lax.psum(jnp.sum(difference * difference), "tensor")
    loss_value = total_error / (student_all.shape[0] * proj_weight.shape[0] * width_count)
    cotangent = difference.astype(jnp.bfloat16)
    proj_grad = lax.dot_general(
        cotangent, student_all, (((0,), (0,)), ((), ())), preferred_element_type=jnp.float32
    )
    row_block = cotangent
    student_grad = lax.psum_scatter(
        jnp.dot(row_block, proj_weight, preferred_element_type=jnp.float32),
        "tensor",
        scatter_dimension=0,
        tiled=True,
    ).astype(jnp.bfloat16)
    return (jnp.reshape(loss_value, (1,)), proj_grad, student_grad)


def solution(mesh):
    placed = (
        P(("groups", "tensor"), None),
        P("tensor", None),
        P("tensor", None),
        P("tensor", None),
        P(),
        P(("groups", "tensor"), None),
        P("tensor", None),
    )
    return jax.shard_map(
        local,
        mesh=mesh,
        in_specs=placed,
        out_specs=(P("groups"), P(("groups", "tensor"), None), P(("groups", "tensor"), None)),
        check_vma=False,
    )
```

profile of v0, /device:TPU:0, one launch (start us, length us, event | category | flops | bytes accessed | tf_op | source)
XLA Modules:
  0.0 371.4 jit_solution(12804801437692001570)
XLA Ops:
  7.2 0.0 copy-start
  7.2 0.0 all-gather.5.cloned.1.call-start
  7.2 0.7 all-gather.5.cloned.1.call-update
  7.9 0.0 reduce-scatter.3.cloned.1.call-start
  8.0 62.5 %all-gather.5.cloned.1.call-done = bf16[512,5376]{1,0:T(8,128)(2,1)} async-done(((bf16[32,5376]{1,0:T(8,128)(2,1)}), bf16[512,5376]{1,0:T(8,128)(2,1)}) %all-gather.5.cloned.1.call-update) | async-done | bytes 5505040 | tf_op jit(solution)/shard_map/all_gather | solution.py:13
  70.4 13.7 %fusion.12 = f32[512,1344]{0,1:T(8,128)} fusion(bf16[512,5376]{1,0:T(8,128)(2,1)} %all-gather.5.cloned.1.call-done, bf16[1344,5376]{1,0:T(8,128)(2,1)} %param.8), kind=kOutput, calls=%fused_computation.19 | convolution fusion | flops 7398752256 | bytes 22708224 | tf_op jit(solution)/shard_map/dot_general | solution.py:14
  84.1 0.0 copy-done.3
  84.1 11.8 %fusion = bf16[512,1344]{0,1:T(8,128)(2,1)S(1)} fusion(bf16[512,5376]{1,0:T(8,128)(2,1)S(1)} %copy-done.3, bf16[1344,5376]{1,0:T(8,128)(2,1)} %param.9, f32[512,1344]{0,1:T(8,128)} %fusion.12), kind=kOutput, calls=%fused_computation.2 | convolution fusion | flops 7405633536 | bytes 24084480 | tf_op jit(solution)/shard_map/dot_general | solution.py:17
  96.0 0.0 slice-done
  96.0 0.0 slice-done.1
  96.0 0.0 slice-done.2
  96.0 11.5 %fusion.13 = f32[512,5376]{1,0:T(8,128)} fusion(bf16[512,1344]{0,1:T(8,128)(2,1)S(1)} %fusion, bf16[1344,5376]{1,0:T(8,128)(2,1)S(1)} %bitcast.18), kind=kOutput, calls=%fused_computation.20 | convolution fusion | flops 7398752256 | bytes 26836992 | tf_op jit(solution)/shard_map/dot_general | solution.py:24
  107.5 0.0 reduce-scatter.3.cloned.1.call-update
  107.5 0.0 all-gather.3.cloned.1.call-start
  107.6 0.7 all-gather.3.cloned.1.call-update
  108.3 0.0 reduce-scatter.5.cloned.1.call-start
  108.4 120.6 %reduce-scatter.3.cloned.1.call-done = f32[32,5376]{1,0:T(8,128)} async-done(((f32[512,5376]{1,0:T(8,128)}), f32[32,5376]{1,0:T(8,128)}) %reduce-scatter.3.cloned.1.call-update) | async-done | bytes 688144 | tf_op jit(solution)/shard_map/reduce_scatter | solution.py:23
  229.0 1.3 multiply_reduce_fusion.1
  230.3 1.3 add_convert_fusion
  231.5 0.6 all_to_all.10
  232.1 0.1 copy.11
  232.2 20.2 %all_to_all.13 = bf16[32,16,336]{2,0,1:T(8,128)(2,1)S(1)} all-to-all(bf16[32,16,336]{2,0,1:T(8,128)(2,1)S(1)} %copy.11), channel_id=1, replica_groups=mesh['groups'=2,'tensor'=16] {'tensor'}, dimensions={1} | all-to-all | bytes 688128 | tf_op jit(solution)/shard_map/all_to_all | solution.py:31
  252.4 0.1 convert_element_type.37
  252.5 0.3 copy.12
  252.7 24.7 %all-gather.3.cloned.1.call-done = bf16[512,2560]{1,0:T(8,128)(2,1)} async-done(((bf16[32,2560]{1,0:T(8,128)(2,1)}), bf16[512,2560]{1,0:T(8,128)(2,1)}) %all-gather.3.cloned.1.call-update) | async-done | bytes 2621456 | tf_op jit(solution)/shard_map/all_gather | solution.py:21
  277.5 3.5 multiply_reduce_fusion
  281.0 3.8 %fusion.8 = f32[512,2560]{1,0:T(8,128)} fusion(bf16[336,2560]{1,0:T(8,128)(2,1)S(1)} %copy-done, bf16[512,336]{0,1:T(8,128)(2,1)S(1)} %get-tuple-element.4), kind=kOutput, calls=%fused_computation.14 | convolution fusion | flops 880803840 | bytes 7307264 | tf_op jit(solution)/shard_map/dot_general | solution.py:44
  284.9 0.0 reduce-scatter.5.cloned.1.call-update
  284.9 32.1 %psum.7 = f32[]{:T(128)} all-reduce(f32[]{:T(128)} %get-tuple-element.3), channel_id=1, replica_groups=mesh['groups'=2,'tensor'=16] {'tensor'}, use_global_device_ids=true, to_apply=%region_3.0 | all-reduce | flops 1 | bytes 8 | tf_op jit(solution)/shard_map/psum | solution.py:36
  317.6 4.6 %fusion.10 = f32[336,2560]{1,0:T(8,128)} fusion(bf16[512,2560]{1,0:T(8,128)(2,1)} %all-gather.3.cloned.1.call-done, bf16[512,336]{0,1:T(8,128)(2,1)S(1)} %get-tuple-element.4), kind=kOutput, calls=%fused_computation.16 | convolution fusion | flops 880803840 | bytes 6406144 | tf_op jit(solution)/shard_map/dot_general | solution.py:39
  322.1 40.0 %reduce-scatter.5.cloned.1.call-done = f32[32,2560]{1,0:T(8,128)} async-done(((f32[512,2560]{1,0:T(8,128)}), f32[32,2560]{1,0:T(8,128)}) %reduce-scatter.5.cloned.1.call-update) | async-done | bytes 327696 | tf_op jit(solution)/shard_map/reduce_scatter | solution.py:43
  362.1 1.7 convert_element_type.35
  (14 shorter events, 0.0 us)
Async XLA Ops:
  7.2 270.3 %copy-start = (bf16[336,2560]{1,0:T(8,128)(2,1)S(1)}, bf16[336,2560]{1,0:T(8,128)(2,1)}, u32[]{:S(2)}) copy-start(bf16[336,2560]{1,0:T(8,128)(2,1)} %param.13) | copy-start | bytes 5160964
  7.2 63.2 %all-gather.5.cloned.1.call-start = ((), (), s32[]{:S(2)}) async-start(), calls=%async_computation.4 | async-start | bytes 5849088 | tf_op jit(solution)/shard_map/all_gather | solution.py:13
  7.9 221.1 %reduce-scatter.3.cloned.1.call-start = ((), (), s32[]{:S(2)}) async-start(), calls=%async_computation.5 | async-start | bytes 11698176 | tf_op jit(solution)/shard_map/reduce_scatter | solution.py:23
  70.4 13.7 %copy-start.3 = (bf16[512,5376]{1,0:T(8,128)(2,1)S(1)}, bf16[512,5376]{1,0:T(8,128)(2,1)}, u32[]{:S(2)}) copy-start(bf16[512,5376]{1,0:T(8,128)(2,1)} %all-gather.5.cloned.1.call-done) | copy-start | bytes 16515076
  70.4 25.6 %slice-start = ((s8[14450688]{0:T(1024)(128)(4,1)}), s8[4194304]{0:T(1024)(128)(4,1)S(1)}, s32[]{:S(2)}) async-start(s8[14450688]{0:T(1024)(128)(4,1)} %bitcast.17), calls=%async_computation.7 | async-start | bytes 8388608
  70.4 25.6 %slice-start.1 = ((s8[14450688]{0:T(1024)(128)(4,1)}), s8[4194304]{0:T(1024)(128)(4,1)S(1)}, s32[]{:S(2)}) async-start(s8[14450688]{0:T(1024)(128)(4,1)} %bitcast.17), calls=%async_computation.8 | async-start | bytes 8388608
  70.4 25.6 %slice-start.2 = ((s8[14450688]{0:T(1024)(128)(4,1)}), s8[4194304]{0:T(1024)(128)(4,1)S(1)}, s32[]{:S(2)}) async-start(s8[14450688]{0:T(1024)(128)(4,1)} %bitcast.17), calls=%async_computation.9 | async-start | bytes 8388608
  84.1 11.9 %slice-start.3 = ((s8[14450688]{0:T(1024)(128)(4,1)}), s8[1867776]{0:T(1024)(128)(4,1)S(1)}, s32[]{:S(2)}) async-start(s8[14450688]{0:T(1024)(128)(4,1)} %bitcast.17), calls=%async_computation.10 | async-start | bytes 3735552
  107.5 0.8 copy-start.2
  107.5 122.7 %copy-start.1 = (bf16[32,5376]{1,0:T(8,128)(2,1)S(1)}, bf16[32,5376]{1,0:T(8,128)(2,1)}, u32[]{:S(2)}) copy-start(bf16[32,5376]{1,0:T(8,128)(2,1)} %param.7) | copy-start | bytes 1032196
  107.5 169.9 %all-gather.3.cloned.1.call-start = ((), (), s32[]{:S(2)}) async-start(), calls=%async_computation.3 | async-start | bytes 2785280 | tf_op jit(solution)/shard_map/all_gather | solution.py:21
  108.3 253.8 %reduce-scatter.5.cloned.1.call-start = ((), (), s32[]{:S(2)}) async-start(), calls=%async_computation.6 | async-start | bytes 5570560 | tf_op jit(solution)/shard_map/reduce_scatter | solution.py:43
Sparse Core Ops, SparseCore 0:
  10.3 60.0 all-gather.4
  107.7 121.2 reduce-scatter.2
  231.5 45.8 all-gather.2
  285.0 77.0 reduce-scatter.4
where the time goes:
time: 372 us; the launch traced here: 371 us
  waiting for transfers between devices  249 us (67%)
  blocking collectives  52.2 us (14%)
  matrix products  48.9 us (13%)
  between operations  15.7 us (4%)
  other arithmetic  4.27 us (1%)
    reduce_scatter x1, waiting for transfers between devices, local(): lax.psum_scatter(jnp.dot(row_block, down_weight, preferred_element_type=j...  121 us
    all_gather x1, waiting for transfers between devices, local(): block_rows = lax.all_gather(teacher_in, 'tensor', axis=0, tiled=True)  62.5 us
    reduce_scatter x1, waiting for transfers between devices, local(): lax.psum_scatter(jnp.dot(row_block, proj_weight, preferred_element_type=j...  40 us
    psum x1, blocking collectives, local(): total_error = lax.psum(jnp.sum(difference * difference), 'tensor')  32.1 us
    all_gather x1, waiting for transfers between devices, local(): student_all = lax.all_gather(student_in, 'tensor', axis=0, tiled=True)  24.7 us
    all_to_all x1, blocking collectives, local(): lax.all_to_all(target_rows, 'tensor', split_axis=1, concat_axis=0, tiled=...  20.2 us
    dot_general x1, matrix products, local(): lax.dot_general(block_rows, gate_weight, contract_last, preferred_element...  13.7 us
    dot_general x1, matrix products, local(): lax.dot_general(block_rows, up_weight, contract_last, preferred_element_t...  11.8 us
  transfers between devices with their start and end apart: 4, of which 4 were waited for; matrix products, arithmetic and copies ran while one was open for 2% of the time, Pallas kernels for 0%

commit v1 on v0

--- a/solution.py
+++ b/solution.py
@@ -6,11 +6,23 @@
 epsilon = 1e-06
 
 
+def gather_around(array, axis, dim):
+    ways, here, step = (lax.axis_size(axis), lax.axis_index(axis), array.shape[dim])
+    dims = [n * ways if d == dim else n for d, n in enumerate(array.shape)]
+    full = lax.dynamic_update_slice_in_dim(
+        jnp.zeros(dims, array.dtype), array, here * step, axis=dim
+    )
+    for far in range(1, ways):
+        array = lax.ppermute(array, axis, [(d, (d + 1) % ways) for d in range(ways)])
+        full = lax.dynamic_update_slice_in_dim(full, array, (here - far) % ways * step, axis=dim)
+    return full
+
+
 def local(teacher_in, gate_weight, up_weight, down_weight, post_gain, student_in, proj_weight):
     width_count = lax.axis_size("tensor")
     gains = post_gain.astype(jnp.float32)
     contract_last = (((1,), (1,)), ((), ()))
-    block_rows = lax.all_gather(teacher_in, "tensor", axis=0, tiled=True)
+    block_rows = gather_around(teacher_in, "tensor", 0)
     gate_value = lax.dot_general(
         block_rows, gate_weight, contract_last, preferred_element_type=jnp.float32
     )

time: 372 us -> 449 us (1.21)
  waiting for transfers between devices: 249 us -> 325 us
    ppermute x0 -> x15, waiting for transfers between devices: none -> 140 us  [gather_around(): lax.ppermute(array, axis, [(d, (d + 1) % ways) for d in range(ways)])]
    all_gather x1 -> x0, waiting for transfers between devices: 62.5 us -> none  [local(): block_rows = lax.all_gather(teacher_in, 'tensor', axis=0, tiled=True)]
  transfers between devices with their start and end apart: 4 -> 18, of which waited for: 4 -> 18; matrix products, arithmetic and copies ran while one was open for 2% -> 2% of each run, Pallas kernels for 0% -> 0%
where the time goes in v1:
time: 449 us
  waiting for transfers between devices  325 us (72%)
  blocking collectives  52.3 us (12%)
  matrix products  48.6 us (11%)
  between operations  15.7 us (3%)
    ppermute x15, waiting for transfers between devices, gather_around(): lax.ppermute(array, axis, [(d, (d + 1) % ways) for d in range(ways)])  140 us
    reduce_scatter x1, waiting for transfers between devices, local(): lax.psum_scatter(jnp.dot(row_block, down_weight, preferred_element_type=j...  120 us
    reduce_scatter x1, waiting for transfers between devices, local(): lax.psum_scatter(jnp.dot(row_block, proj_weight, preferred_element_type=j...  39.9 us
    psum x1, blocking collectives, local(): total_error = lax.psum(jnp.sum(difference * difference), 'tensor')  32.1 us
    all_gather x1, waiting for transfers between devices, local(): student_all = lax.all_gather(student_in, 'tensor', axis=0, tiled=True)  24.7 us
    all_to_all x1, blocking collectives, local(): lax.all_to_all(target_rows, 'tensor', split_axis=1, concat_axis=0, tiled=...  20.2 us
    dot_general x1, matrix products, local(): jnp.dot(row_block, down_weight, preferred_element_type=jnp.float32)  13.9 us
    dot_general x1, matrix products, local(): lax.dot_general(block_rows, up_weight, contract_last, preferred_element_t...  12.1 us
  transfers between devices with their start and end apart: 18, of which 18 were waited for; matrix products, arithmetic and copies ran while one was open for 2% of the time, Pallas kernels for 0%

profile of v1, /device:TPU:0, one launch (start us, length us, event | category | flops | bytes accessed | tf_op | source)
XLA Modules:
  0.0 448.9 jit_solution(9977629862394994753)
XLA Ops:
  7.2 0.5 collective-permute-start
  8.3 9.6 %collective-permute-done = bf16[32,5376]{1,0:T(8,128)(2,1)S(1)} collective-permute-done((bf16[32,5376]{1,0:T(8,128)(2,1)}, bf16[32,5376]{1,0:T(8,128)(2,1)S(1)}, u32[]{:S(2)}, u32[]{:S(2)}) %collective-permute-start) | collective-permute-done | bytes 344096 | tf_op jit(solution)/shard_map/ppermute | solution.py:16
  17.9 9.3 %collective-permute-done.1 = bf16[32,5376]{1,0:T(8,128)(2,1)S(1)} collective-permute-done((bf16[32,5376]{1,0:T(8,128)(2,1)S(1)}, bf16[32,5376]{1,0:T(8,128)(2,1)S(1)}, u32[]{:S(2)}, u32[]{:S(2)}) %collective-permute-start.1) | collective-permute-done | bytes 344096 | tf_op jit(solution)/shard_map/ppermute | solution.py:16
  27.3 9.3 %collective-permute-done.2 = bf16[32,5376]{1,0:T(8,128)(2,1)S(1)} collective-permute-done((bf16[32,5376]{1,0:T(8,128)(2,1)S(1)}, bf16[32,5376]{1,0:T(8,128)(2,1)S(1)}, u32[]{:S(2)}, u32[]{:S(2)}) %collective-permute-start.2) | collective-permute-done | bytes 344096 | tf_op jit(solution)/shard_map/ppermute | solution.py:16
  36.7 9.3 %collective-permute-done.3 = bf16[32,5376]{1,0:T(8,128)(2,1)S(1)} collective-permute-done((bf16[32,5376]{1,0:T(8,128)(2,1)S(1)}, bf16[32,5376]{1,0:T(8,128)(2,1)S(1)}, u32[]{:S(2)}, u32[]{:S(2)}) %collective-permute-start.3) | collective-permute-done | bytes 344096 | tf_op jit(solution)/shard_map/ppermute | solution.py:16
  46.0 9.3 %collective-permute-done.4 = bf16[32,5376]{1,0:T(8,128)(2,1)S(1)} collective-permute-done((bf16[32,5376]{1,0:T(8,128)(2,1)S(1)}, bf16[32,5376]{1,0:T(8,128)(2,1)S(1)}, u32[]{:S(2)}, u32[]{:S(2)}) %collective-permute-start.4) | collective-permute-done | bytes 344096 | tf_op jit(solution)/shard_map/ppermute | solution.py:16
  55.4 9.3 %collective-permute-done.5 = bf16[32,5376]{1,0:T(8,128)(2,1)S(1)} collective-permute-done((bf16[32,5376]{1,0:T(8,128)(2,1)S(1)}, bf16[32,5376]{1,0:T(8,128)(2,1)S(1)}, u32[]{:S(2)}, u32[]{:S(2)}) %collective-permute-start.5) | collective-permute-done | bytes 344096 | tf_op jit(solution)/shard_map/ppermute | solution.py:16
  64.8 9.3 %collective-permute-done.6 = bf16[32,5376]{1,0:T(8,128)(2,1)S(1)} collective-permute-done((bf16[32,5376]{1,0:T(8,128)(2,1)S(1)}, bf16[32,5376]{1,0:T(8,128)(2,1)S(1)}, u32[]{:S(2)}, u32[]{:S(2)}) %collective-permute-start.6) | collective-permute-done | bytes 344096 | tf_op jit(solution)/shard_map/ppermute | solution.py:16
  74.1 9.3 %collective-permute-done.7 = bf16[32,5376]{1,0:T(8,128)(2,1)S(1)} collective-permute-done((bf16[32,5376]{1,0:T(8,128)(2,1)S(1)}, bf16[32,5376]{1,0:T(8,128)(2,1)S(1)}, u32[]{:S(2)}, u32[]{:S(2)}) %collective-permute-start.7) | collective-permute-done | bytes 344096 | tf_op jit(solution)/shard_map/ppermute | solution.py:16
  83.5 9.3 %collective-permute-done.8 = bf16[32,5376]{1,0:T(8,128)(2,1)S(1)} collective-permute-done((bf16[32,5376]{1,0:T(8,128)(2,1)S(1)}, bf16[32,5376]{1,0:T(8,128)(2,1)S(1)}, u32[]{:S(2)}, u32[]{:S(2)}) %collective-permute-start.8) | collective-permute-done | bytes 344096 | tf_op jit(solution)/shard_map/ppermute | solution.py:16
  92.9 9.3 %collective-permute-done.9 = bf16[32,5376]{1,0:T(8,128)(2,1)S(1)} collective-permute-done((bf16[32,5376]{1,0:T(8,128)(2,1)S(1)}, bf16[32,5376]{1,0:T(8,128)(2,1)S(1)}, u32[]{:S(2)}, u32[]{:S(2)}) %collective-permute-start.9) | collective-permute-done | bytes 344096 | tf_op jit(solution)/shard_map/ppermute | solution.py:16
  102.3 9.3 %collective-permute-done.10 = bf16[32,5376]{1,0:T(8,128)(2,1)S(1)} collective-permute-done((bf16[32,5376]{1,0:T(8,128)(2,1)S(1)}, bf16[32,5376]{1,0:T(8,128)(2,1)S(1)}, u32[]{:S(2)}, u32[]{:S(2)}) %collective-permute-start.10) | collective-permute-done | bytes 344096 | tf_op jit(solution)/shard_map/ppermute | solution.py:16
  111.6 9.3 %collective-permute-done.11 = bf16[32,5376]{1,0:T(8,128)(2,1)S(1)} collective-permute-done((bf16[32,5376]{1,0:T(8,128)(2,1)S(1)}, bf16[32,5376]{1,0:T(8,128)(2,1)S(1)}, u32[]{:S(2)}, u32[]{:S(2)}) %collective-permute-start.11) | collective-permute-done | bytes 344096 | tf_op jit(solution)/shard_map/ppermute | solution.py:16
  121.0 9.3 %collective-permute-done.12 = bf16[32,5376]{1,0:T(8,128)(2,1)S(1)} collective-permute-done((bf16[32,5376]{1,0:T(8,128)(2,1)S(1)}, bf16[32,5376]{1,0:T(8,128)(2,1)S(1)}, u32[]{:S(2)}, u32[]{:S(2)}) %collective-permute-start.12) | collective-permute-done | bytes 344096 | tf_op jit(solution)/shard_map/ppermute | solution.py:16
  130.4 9.3 %collective-permute-done.13 = bf16[32,5376]{1,0:T(8,128)(2,1)S(1)} collective-permute-done((bf16[32,5376]{1,0:T(8,128)(2,1)S(1)}, bf16[32,5376]{1,0:T(8,128)(2,1)S(1)}, u32[]{:S(2)}, u32[]{:S(2)}) %collective-permute-start.13) | collective-permute-done | bytes 344096 | tf_op jit(solution)/shard_map/ppermute | solution.py:16
  139.8 9.3 %collective-permute-done.14 = bf16[32,5376]{1,0:T(8,128)(2,1)S(1)} collective-permute-done((bf16[32,5376]{1,0:T(8,128)(2,1)S(1)}, bf16[32,5376]{1,0:T(8,128)(2,1)S(1)}, u32[]{:S(2)}, u32[]{:S(2)}) %collective-permute-start.14) | collective-permute-done | bytes 344096 | tf_op jit(solution)/shard_map/ppermute | solution.py:16
  149.1 10.6 %fusion.23 = f32[512,1344]{0,1:T(8,128)S(1)} fusion(bf16[512,5376]{1,0:T(8,128)(2,1)S(1)} %constant_dynamic-update-slice_fusion, bf16[1344,5376]{1,0:T(8,128)(2,1)} %param.8), kind=kOutput, calls=%fused_computation.44 | convolution fusion | flops 7398752256 | bytes 22708224 | tf_op jit(solution)/shard_map/dot_general | solution.py:26
  159.8 12.1 %fusion.24 = f32[512,1344]{0,1:T(8,128)} fusion(bf16[512,5376]{1,0:T(8,128)(2,1)S(1)} %constant_dynamic-update-slice_fusion, bf16[1344,5376]{1,0:T(8,128)(2,1)} %param.9), kind=kOutput, calls=%fused_computation.45 | convolution fusion | flops 7398752256 | bytes 22708224 | tf_op jit(solution)/shard_map/dot_general | solution.py:29
  171.9 13.9 %fusion.9 = f32[512,5376]{1,0:T(8,128)} fusion(bf16[1344,5376]{1,0:T(8,128)(2,1)S(1)} %bitcast.16, f32[512,1344]{0,1:T(8,128)} %fusion.24, f32[512,1344]{0,1:T(8,128)S(1)} %fusion.23), kind=kOutput, calls=%fused_computation.10 | convolution fusion | flops 7405633536 | bytes 30965760 | tf_op jit(solution)/shard_map/dot_general | solution.py:36
  185.9 0.7 all-gather.2.cloned.1.call-update
  186.9 119.6 %reduce-scatter.3.cloned.1.call-done = f32[32,5376]{1,0:T(8,128)} async-done(((f32[512,5376]{1,0:T(8,128)}), f32[32,5376]{1,0:T(8,128)}) %reduce-scatter.3.cloned.1.call-update) | async-done | bytes 688144 | tf_op jit(solution)/shard_map/reduce_scatter | solution.py:35
  306.4 1.3 multiply_reduce_fusion.1
  307.7 1.3 add_convert_fusion
  309.0 0.6 all_to_all.10
  309.7 20.2 %all_to_all.13 = bf16[32,16,336]{2,0,1:T(8,128)(2,1)S(1)} all-to-all(bf16[32,16,336]{2,0,1:T(8,128)(2,1)S(1)} %copy.11), channel_id=1, replica_groups=mesh['groups'=2,'tensor'=16] {'tensor'}, dimensions={1} | all-to-all | bytes 688128 | tf_op jit(solution)/shard_map/all_to_all | solution.py:43
  330.2 24.7 %all-gather.2.cloned.1.call-done = bf16[512,2560]{1,0:T(8,128)(2,1)} async-done(((bf16[32,2560]{1,0:T(8,128)(2,1)}), bf16[512,2560]{1,0:T(8,128)(2,1)}) %all-gather.2.cloned.1.call-update) | async-done | bytes 2621456 | tf_op jit(solution)/shard_map/all_gather | solution.py:33
  354.9 3.5 multiply_reduce_fusion
  358.5 3.9 fusion.15
  362.4 32.1 %psum.7 = f32[]{:T(128)} all-reduce(f32[]{:T(128)} %get-tuple-element.3), channel_id=1, replica_groups=mesh['groups'=2,'tensor'=16] {'tensor'}, use_global_device_ids=true, to_apply=%region_3.4 | all-reduce | flops 1 | bytes 8 | tf_op jit(solution)/shard_map/psum | solution.py:48
  395.1 4.6 %fusion.17 = f32[336,2560]{1,0:T(8,128)} fusion(bf16[512,2560]{1,0:T(8,128)(2,1)} %all-gather.2.cloned.1.call-done, bf16[512,336]{0,1:T(8,128)(2,1)S(1)} %get-tuple-element.4), kind=kOutput, calls=%fused_computation.21 | convolution fusion | flops 880803840 | bytes 6406144 | tf_op jit(solution)/shard_map/dot_general | solution.py:51
  399.6 39.9 %reduce-scatter.5.cloned.1.call-done = f32[32,2560]{1,0:T(8,128)} async-done(((f32[512,2560]{1,0:T(8,128)}), f32[32,2560]{1,0:T(8,128)}) %reduce-scatter.5.cloned.1.call-update) | async-done | bytes 327696 | tf_op jit(solution)/shard_map/reduce_scatter | solution.py:55
  439.6 1.7 convert_element_type.35
  (56 shorter events, 1.8 us)
Async XLA Ops:
  7.2 347.8 %copy-start = (bf16[336,2560]{1,0:T(8,128)(2,1)S(1)}, bf16[336,2560]{1,0:T(8,128)(2,1)}, u32[]{:S(2)}) copy-start(bf16[336,2560]{1,0:T(8,128)(2,1)} %param.13) | copy-start | bytes 5160964
  7.2 1.1 copy-start.1
  7.2 299.3 %reduce-scatter.3.cloned.1.call-start = ((), (), s32[]{:S(2)}) async-start(), calls=%async_computation.4 | async-start | bytes 11698176 | tf_op jit(solution)/shard_map/reduce_scatter | solution.py:35
  7.2 10.6 %collective-permute-start = (bf16[32,5376]{1,0:T(8,128)(2,1)}, bf16[32,5376]{1,0:T(8,128)(2,1)S(1)}, u32[]{:S(2)}, u32[]{:S(2)}) collective-permute-start(bf16[32,5376]{1,0:T(8,128)(2,1)} %param.7), channel_id=1, source_target_pairs={{0,1},{1,2},{2,3},{3,4},{4,5},{5,6},{6,7},{7,8},{8,9},{9,10},{10,1... | collective-permute-start | bytes 1032200 | tf_op jit(solution)/shard_map/ppermute | solution.py:16
  17.9 9.4 %collective-permute-start.1 = (bf16[32,5376]{1,0:T(8,128)(2,1)S(1)}, bf16[32,5376]{1,0:T(8,128)(2,1)S(1)}, u32[]{:S(2)}, u32[]{:S(2)}) collective-permute-start(bf16[32,5376]{1,0:T(8,128)(2,1)S(1)} %collective-permute-done), channel_id=1, source_target_pairs={{0,1},{1,2},{2,3},{3,4},{4,5},{5,6},{6,7},{7,8},{8,9},{9,10},{10,1... | collective-permute-start | bytes 1032200 | tf_op jit(solution)/shard_map/ppermute | solution.py:16
  27.2 9.4 %collective-permute-start.2 = (bf16[32,5376]{1,0:T(8,128)(2,1)S(1)}, bf16[32,5376]{1,0:T(8,128)(2,1)S(1)}, u32[]{:S(2)}, u32[]{:S(2)}) collective-permute-start(bf16[32,5376]{1,0:T(8,128)(2,1)S(1)} %collective-permute-done.1), channel_id=1, source_target_pairs={{0,1},{1,2},{2,3},{3,4},{4,5},{5,6},{6,7},{7,8},{8,9},{9,10},{10,1... | collective-permute-start | bytes 1032200 | tf_op jit(solution)/shard_map/ppermute | solution.py:16
  36.6 9.4 %collective-permute-start.3 = (bf16[32,5376]{1,0:T(8,128)(2,1)S(1)}, bf16[32,5376]{1,0:T(8,128)(2,1)S(1)}, u32[]{:S(2)}, u32[]{:S(2)}) collective-permute-start(bf16[32,5376]{1,0:T(8,128)(2,1)S(1)} %collective-permute-done.2), channel_id=1, source_target_pairs={{0,1},{1,2},{2,3},{3,4},{4,5},{5,6},{6,7},{7,8},{8,9},{9,10},{10,1... | collective-permute-start | bytes 1032200 | tf_op jit(solution)/shard_map/ppermute | solution.py:16
  46.0 9.4 %collective-permute-start.4 = (bf16[32,5376]{1,0:T(8,128)(2,1)S(1)}, bf16[32,5376]{1,0:T(8,128)(2,1)S(1)}, u32[]{:S(2)}, u32[]{:S(2)}) collective-permute-start(bf16[32,5376]{1,0:T(8,128)(2,1)S(1)} %collective-permute-done.3), channel_id=1, source_target_pairs={{0,1},{1,2},{2,3},{3,4},{4,5},{5,6},{6,7},{7,8},{8,9},{9,10},{10,1... | collective-permute-start | bytes 1032200 | tf_op jit(solution)/shard_map/ppermute | solution.py:16
  55.4 9.4 %collective-permute-start.5 = (bf16[32,5376]{1,0:T(8,128)(2,1)S(1)}, bf16[32,5376]{1,0:T(8,128)(2,1)S(1)}, u32[]{:S(2)}, u32[]{:S(2)}) collective-permute-start(bf16[32,5376]{1,0:T(8,128)(2,1)S(1)} %collective-permute-done.4), channel_id=1, source_target_pairs={{0,1},{1,2},{2,3},{3,4},{4,5},{5,6},{6,7},{7,8},{8,9},{9,10},{10,1... | collective-permute-start | bytes 1032200 | tf_op jit(solution)/shard_map/ppermute | solution.py:16
  64.7 9.4 %collective-permute-start.6 = (bf16[32,5376]{1,0:T(8,128)(2,1)S(1)}, bf16[32,5376]{1,0:T(8,128)(2,1)S(1)}, u32[]{:S(2)}, u32[]{:S(2)}) collective-permute-start(bf16[32,5376]{1,0:T(8,128)(2,1)S(1)} %collective-permute-done.5), channel_id=1, source_target_pairs={{0,1},{1,2},{2,3},{3,4},{4,5},{5,6},{6,7},{7,8},{8,9},{9,10},{10,1... | collective-permute-start | bytes 1032200 | tf_op jit(solution)/shard_map/ppermute | solution.py:16
  74.1 9.4 %collective-permute-start.7 = (bf16[32,5376]{1,0:T(8,128)(2,1)S(1)}, bf16[32,5376]{1,0:T(8,128)(2,1)S(1)}, u32[]{:S(2)}, u32[]{:S(2)}) collective-permute-start(bf16[32,5376]{1,0:T(8,128)(2,1)S(1)} %collective-permute-done.6), channel_id=1, source_target_pairs={{0,1},{1,2},{2,3},{3,4},{4,5},{5,6},{6,7},{7,8},{8,9},{9,10},{10,1... | collective-permute-start | bytes 1032200 | tf_op jit(solution)/shard_map/ppermute | solution.py:16
  83.5 9.4 %collective-permute-start.8 = (bf16[32,5376]{1,0:T(8,128)(2,1)S(1)}, bf16[32,5376]{1,0:T(8,128)(2,1)S(1)}, u32[]{:S(2)}, u32[]{:S(2)}) collective-permute-start(bf16[32,5376]{1,0:T(8,128)(2,1)S(1)} %collective-permute-done.7), channel_id=1, source_target_pairs={{0,1},{1,2},{2,3},{3,4},{4,5},{5,6},{6,7},{7,8},{8,9},{9,10},{10,1... | collective-permute-start | bytes 1032200 | tf_op jit(solution)/shard_map/ppermute | solution.py:16
  92.9 9.4 %collective-permute-start.9 = (bf16[32,5376]{1,0:T(8,128)(2,1)S(1)}, bf16[32,5376]{1,0:T(8,128)(2,1)S(1)}, u32[]{:S(2)}, u32[]{:S(2)}) collective-permute-start(bf16[32,5376]{1,0:T(8,128)(2,1)S(1)} %collective-permute-done.8), channel_id=1, source_target_pairs={{0,1},{1,2},{2,3},{3,4},{4,5},{5,6},{6,7},{7,8},{8,9},{9,10},{10,1... | collective-permute-start | bytes 1032200 | tf_op jit(solution)/shard_map/ppermute | solution.py:16
  102.2 9.4 %collective-permute-start.10 = (bf16[32,5376]{1,0:T(8,128)(2,1)S(1)}, bf16[32,5376]{1,0:T(8,128)(2,1)S(1)}, u32[]{:S(2)}, u32[]{:S(2)}) collective-permute-start(bf16[32,5376]{1,0:T(8,128)(2,1)S(1)} %collective-permute-done.9), channel_id=1, source_target_pairs={{0,1},{1,2},{2,3},{3,4},{4,5},{5,6},{6,7},{7,8},{8,9},{9,10},{10,1... | collective-permute-start | bytes 1032200 | tf_op jit(solution)/shard_map/ppermute | solution.py:16
  111.6 9.4 %collective-permute-start.11 = (bf16[32,5376]{1,0:T(8,128)(2,1)S(1)}, bf16[32,5376]{1,0:T(8,128)(2,1)S(1)}, u32[]{:S(2)}, u32[]{:S(2)}) collective-permute-start(bf16[32,5376]{1,0:T(8,128)(2,1)S(1)} %collective-permute-done.10), channel_id=1, source_target_pairs={{0,1},{1,2},{2,3},{3,4},{4,5},{5,6},{6,7},{7,8},{8,9},{9,10},{10,1... | collective-permute-start | bytes 1032200 | tf_op jit(solution)/shard_map/ppermute | solution.py:16
  121.0 9.4 %collective-permute-start.12 = (bf16[32,5376]{1,0:T(8,128)(2,1)S(1)}, bf16[32,5376]{1,0:T(8,128)(2,1)S(1)}, u32[]{:S(2)}, u32[]{:S(2)}) collective-permute-start(bf16[32,5376]{1,0:T(8,128)(2,1)S(1)} %collective-permute-done.11), channel_id=1, source_target_pairs={{0,1},{1,2},{2,3},{3,4},{4,5},{5,6},{6,7},{7,8},{8,9},{9,10},{10,1... | collective-permute-start | bytes 1032200 | tf_op jit(solution)/shard_map/ppermute | solution.py:16
  130.3 9.4 %collective-permute-start.13 = (bf16[32,5376]{1,0:T(8,128)(2,1)S(1)}, bf16[32,5376]{1,0:T(8,128)(2,1)S(1)}, u32[]{:S(2)}, u32[]{:S(2)}) collective-permute-start(bf16[32,5376]{1,0:T(8,128)(2,1)S(1)} %collective-permute-done.12), channel_id=1, source_target_pairs={{0,1},{1,2},{2,3},{3,4},{4,5},{5,6},{6,7},{7,8},{8,9},{9,10},{10,1... | collective-permute-start | bytes 1032200 | tf_op jit(solution)/shard_map/ppermute | solution.py:16
  139.7 9.4 %collective-permute-start.14 = (bf16[32,5376]{1,0:T(8,128)(2,1)S(1)}, bf16[32,5376]{1,0:T(8,128)(2,1)S(1)}, u32[]{:S(2)}, u32[]{:S(2)}) collective-permute-start(bf16[32,5376]{1,0:T(8,128)(2,1)S(1)} %collective-permute-done.13), channel_id=1, source_target_pairs={{0,1},{1,2},{2,3},{3,4},{4,5},{5,6},{6,7},{7,8},{8,9},{9,10},{10,1... | collective-permute-start | bytes 1032200 | tf_op jit(solution)/shard_map/ppermute | solution.py:16
  149.1 22.8 %slice-start = ((s8[14450688]{0:T(1024)(128)(4,1)}), s8[4194304]{0:T(1024)(128)(4,1)S(1)}, s32[]{:S(2)}) async-start(s8[14450688]{0:T(1024)(128)(4,1)} %bitcast.15), calls=%async_computation.6 | async-start | bytes 8388608
  149.1 22.8 %slice-start.1 = ((s8[14450688]{0:T(1024)(128)(4,1)}), s8[4194304]{0:T(1024)(128)(4,1)S(1)}, s32[]{:S(2)}) async-start(s8[14450688]{0:T(1024)(128)(4,1)} %bitcast.15), calls=%async_computation.7 | async-start | bytes 8388608
  159.7 12.2 %slice-start.2 = ((s8[14450688]{0:T(1024)(128)(4,1)}), s8[4194304]{0:T(1024)(128)(4,1)S(1)}, s32[]{:S(2)}) async-start(s8[14450688]{0:T(1024)(128)(4,1)} %bitcast.15), calls=%async_computation.8 | async-start | bytes 8388608
  159.8 12.2 %slice-start.3 = ((s8[14450688]{0:T(1024)(128)(4,1)}), s8[1867776]{0:T(1024)(128)(4,1)S(1)}, s32[]{:S(2)}) async-start(s8[14450688]{0:T(1024)(128)(4,1)} %bitcast.15), calls=%async_computation.9 | async-start | bytes 3735552
  185.8 1.0 copy-start.2
  185.9 169.1 %all-gather.2.cloned.1.call-start = ((), (), s32[]{:S(2)}) async-start(), calls=%async_computation.3 | async-start | bytes 2785280 | tf_op jit(solution)/shard_map/all_gather | solution.py:33
  186.6 252.9 %reduce-scatter.5.cloned.1.call-start = ((), (), s32[]{:S(2)}) async-start(), calls=%async_computation.5 | async-start | bytes 5570560 | tf_op jit(solution)/shard_map/reduce_scatter | solution.py:55
Sparse Core Ops, SparseCore 0:
  186.0 120.4 reduce-scatter.2
  309.0 45.9 all-gather.1
  362.5 77.0 reduce-scatter.4
